TPU v7x, 32 devices: a whole 2x2x4 slice. The times are simulated.
32 devices in a mesh: region: 2 (over x), row: 4 (over y, core), col: 4 (over z).
Axes of the slice: x: 2, y: 2, z: 4, core: 2. Of those that a mesh axis runs over, the one named last changes fastest.
Arguments:
- queries: bfloat16 [256, 32, 768], P(('region', 'row'), 'col'), parts along dimension 0, may hold values from -16 to 16
- key_states: bfloat16 [256, 32, 768], P(('region', 'row'), 'col'), parts along dimension 0, may hold values from -16 to 16
- value_states: bfloat16 [256, 32, 768], P(('region', 'row'), 'col'), parts along dimension 0, may hold values from -6 to 6
- out_grad: bfloat16 [256, 32, 768], P(('region', 'row'), 'col'), parts along dimension 0, may hold values from -6 to 6
- tissue: int32 [32, 4], P('region'), parts along dimension 0, may hold values from 0 to 1, as said below
- slide_id: int32 [32, 4], P('region'), parts along dimension 0, may hold values from 0 to 2, never falling along the last dimension, each value on 1 to 2 neighbouring positions
Outputs:
- attended: bfloat16 [256, 32, 768], P(('region', 'row'), 'col'), parts along dimension 0
- query_grad: bfloat16 [256, 32, 768], P(('region', 'row'), 'col'), parts along dimension 0
- key_grad: bfloat16 [256, 32, 768], P(('region', 'row'), 'col'), parts along dimension 0
- value_grad: bfloat16 [256, 32, 768], P(('region', 'row'), 'col'), parts along dimension 0
There are 2 independent parts, one for each index of `region`. A program takes and returns all parts, laid end to end along the dimension named above; each array names one. Nothing has to cross between parts.
Inputs may be any that keep to these rules, and one draw needn't show every extreme that they name: 1 marks a block of tissue.
All inputs are finite; a program needn't handle non-finite values.
Results may differ from a plain program's by a relative error of at most 0.015.
Values may be sent and summed in bfloat16 or wider, within the bound.
A program may use at most 64 MiB of HBM per device.

v0:
```python
import math

import jax
import jax.numpy as jnp
import numpy as np
from jax import lax
from jax.sharding import PartitionSpec as P

HEADS = 12


def shifted(block, axis, distance):
    devices = range(lax.axis_size(axis))
    route = [(i - distance, i) for i in devices if i - distance in devices]
    return lax.ppermute(block, axis, route)


def extended_2(array, sides, width):
    for axis, dim in sides:
        size, length = (lax.axis_size(axis), array.shape[dim])
        up = [(i, (i + 1) % size) for i in range(size - 1)]
        down = [(j, i) for i, j in up]
        last = lax.slice_in_dim(array, length - width, length, axis=dim)
        leading = lax.slice_in_dim(array, 0, width, axis=dim)
        before = lax.ppermute(last, axis, up)
        after = lax.ppermute(leading, axis, down)
        array = jnp.concatenate([before, array, after], axis=dim)
    return array


def window_tables(tile_cols):
    padded_cols = tile_cols + 16
    center = np.arange(8 * tile_cols)
    region = np.arange(16 * padded_cols)
    row_offset = (center // tile_cols)[:, None] + 4 - (region // padded_cols)[None, :]
    col_offset = (center % tile_cols)[:, None] + 4 - (region % padded_cols)[None, :]
    window = (np.abs(row_offset) <= 3) & (np.abs(col_offset) <= 3)
    itself = (row_offset == 0) & (col_offset == 0)
    return (jnp.asarray(window), jnp.asarray(itself))


def token_labels(table, fill_value, row_start, col_start, tile_rows, tile_cols):
    padded = jnp.pad(table, ((1, 1), (1, 2)), constant_values=fill_value)
    blocks = lax.dynamic_slice(
        padded, (row_start // 8, col_start // 8), (tile_rows // 8 + 2, tile_cols // 8 + 3)
    )
    tokens = jnp.repeat(jnp.repeat(blocks, 8, axis=0), 8, axis=1)
    return tokens[4 : tile_rows + 12, 4 : tile_cols + 20]


def to_heads(array):
    rows, cols, feature = array.shape
    return array.reshape(rows, cols, HEADS, feature // HEADS).transpose(2, 0, 1, 3)


def from_heads(array):
    heads, rows, cols, depth = array.shape
    return array.transpose(1, 2, 0, 3).reshape(rows, cols, heads * depth)


def extend_rim(extended, first_dim, rim_size):
    padding = [(0, 0)] * extended.ndim
    padding[first_dim] = (4 - rim_size, 4 - rim_size)
    padding[first_dim + 1] = (4 - rim_size, 12 - rim_size)
    return jnp.pad(extended, padding)


def block_mask(labels, row_first, tile_cols, window, itself):
    tissue_ext, slide_ext = labels
    padded_cols = tile_cols + 16
    center_tis = lax.dynamic_slice(tissue_ext, (row_first + 4, 4), (8, tile_cols)).reshape(
        8 * tile_cols
    )
    center_sid = lax.dynamic_slice(slide_ext, (row_first + 4, 4), (8, tile_cols)).reshape(
        8 * tile_cols
    )
    region_tis = lax.dynamic_slice(tissue_ext, (row_first, 0), (16, padded_cols)).reshape(
        16 * padded_cols
    )
    region_sid = lax.dynamic_slice(slide_ext, (row_first, 0), (16, padded_cols)).reshape(
        16 * padded_cols
    )
    paired = (
        (center_tis[:, None] == 1)
        & (region_tis[None, :] == 1)
        & (center_sid[:, None] == region_sid[None, :])
    )
    return (itself | window & paired, jnp.any(center_tis == 1))


def row_block(array, row_first):
    heads, rows, cols, depth = array.shape
    return lax.dynamic_slice(array, (0, row_first, 0, 0), (heads, 8, cols, depth)).reshape(
        heads, 8 * cols, depth
    )


def query_center(row_first, inputs):
    query_heads, grad_heads, key_value_ext, labels, window, itself, score_scale = inputs
    heads, rows, tile_cols, depth = query_heads.shape
    padded_cols = tile_cols + 16
    allowed, live = block_mask(labels, row_first, tile_cols, window, itself)
    query_blk = row_block(query_heads, row_first)
    grad_blk = row_block(grad_heads, row_first)
    region = lax.dynamic_slice(
        key_value_ext, (0, 0, row_first, 0, 0), (2, heads, 16, padded_cols, depth)
    )
    key_reg = region[0].reshape(heads, 16 * padded_cols, depth)
    value_reg = region[1].reshape(heads, 16 * padded_cols, depth)
    scores = (
        jnp.einsum("hqd,hkd->hqk", query_blk, key_reg, preferred_element_type=jnp.float32)
        * score_scale
    )
    pattern = allowed[None]
    row_top = jnp.max(jnp.where(pattern, scores, -jnp.inf), axis=2, keepdims=True)
    row_total = jnp.sum(
        jnp.exp(jnp.where(pattern, scores - row_top, -jnp.inf)), axis=2, keepdims=True
    )
    log_total = row_top + jnp.log(row_total)
    weights = jnp.exp(jnp.where(pattern, scores - log_total, -jnp.inf))
    soft_weights = weights.astype(jnp.bfloat16)
    attended = jnp.einsum(
        "hqk,hkd->hqd", soft_weights, value_reg, preferred_element_type=jnp.float32
    ).astype(jnp.bfloat16)
    row_delta = jnp.einsum("hqd,hqd->hq", grad_blk, attended, preferred_element_type=jnp.float32)
    prob_grad = jnp.einsum("hqd,hkd->hqk", grad_blk, value_reg, preferred_element_type=jnp.float32)
    score_grad = (weights * (prob_grad - row_delta[:, :, None]) * score_scale).astype(jnp.bfloat16)
    query_grad = jnp.einsum(
        "hqk,hkd->hqd", score_grad, key_reg, preferred_element_type=jnp.float32
    ).astype(jnp.bfloat16)
    results = (attended, query_grad, log_total[:, :, 0], row_delta)
    key_part = jnp.einsum("hqk,hqd->hkd", score_grad, query_blk, preferred_element_type=jnp.float32)
    value_part = jnp.einsum(
        "hqk,hqd->hkd", soft_weights, grad_blk, preferred_element_type=jnp.float32
    )
    return results + (jnp.stack([key_part, value_part]),)


def return_rims(grads_ext, tile_rows, tile_cols):
    from_east = shifted(grads_ext[:, :, :, 0:4].astype(jnp.bfloat16), "col", -1).astype(jnp.float32)
    from_west = shifted(
        grads_ext[:, :, :, tile_cols + 4 : tile_cols + 8].astype(jnp.bfloat16), "col", 1
    ).astype(jnp.float32)
    grads_ext = grads_ext.at[:, :, :, tile_cols : tile_cols + 4].add(from_east)
    grads_ext = grads_ext.at[:, :, :, 4:8].add(from_west)
    from_south = shifted(
        grads_ext[:, :, 0:4, 4 : tile_cols + 4].astype(jnp.bfloat16), "row", -1
    ).astype(jnp.float32)
    from_north = shifted(
        grads_ext[:, :, tile_rows + 4 : tile_rows + 8, 4 : tile_cols + 4].astype(jnp.bfloat16),
        "row",
        1,
    ).astype(jnp.float32)
    interior = grads_ext[:, :, 4 : tile_rows + 4, 4 : tile_cols + 4]
    interior = interior.at[:, :, tile_rows - 4 : tile_rows].add(from_south)
    interior = interior.at[:, :, 0:4].add(from_north)
    return (
        from_heads(interior[0]).astype(jnp.bfloat16),
        from_heads(interior[1]).astype(jnp.bfloat16),
    )


def local(queries, key_states, value_states, out_grad, tissue, slide_id):
    tile_rows, tile_cols, feature = queries.shape
    depth = feature // HEADS
    padded_cols = tile_cols + 16
    score_scale = 1.0 / math.sqrt(depth)
    rim_size = 4
    row_start = lax.axis_index("row") * tile_rows
    col_start = lax.axis_index("col") * tile_cols
    labels = (
        token_labels(tissue, 0, row_start, col_start, tile_rows, tile_cols),
        token_labels(slide_id, -1, row_start, col_start, tile_rows, tile_cols),
    )
    window, itself = window_tables(tile_cols)
    query_heads = to_heads(queries)
    grad_heads = to_heads(out_grad)
    key_heads = to_heads(key_states)
    value_heads = to_heads(value_states)
    key_value_ext = extended_2(
        jnp.stack([key_heads, value_heads]), (("row", 2), ("col", 3)), rim_size
    )
    key_value_ext = extend_rim(key_value_ext, 2, rim_size)
    block_count = tile_rows // 8
    inputs = (query_heads, grad_heads, key_value_ext, labels, window, itself, score_scale)
    initial = (
        jnp.zeros((HEADS, tile_rows, tile_cols, depth), jnp.bfloat16),
        jnp.zeros((HEADS, tile_rows, tile_cols, depth), jnp.bfloat16),
        jnp.zeros((2, HEADS, tile_rows, tile_cols), jnp.float32),
    )
    initial = initial + (jnp.zeros((2, HEADS, tile_rows + 8, padded_cols, depth), jnp.float32),)

    def query_step(block_index, running):
        row_first = block_index * 8
        results = query_center(row_first, inputs)
        corner = (0, row_first, 0, 0)
        attended = lax.dynamic_update_slice(
            running[0], results[0].reshape(HEADS, 8, tile_cols, depth), corner
        )
        query_grad = lax.dynamic_update_slice(
            running[1], results[1].reshape(HEADS, 8, tile_cols, depth), corner
        )
        stat_blk = jnp.stack([results[2], results[3]]).reshape(2, HEADS, 8, tile_cols)
        stats = lax.dynamic_update_slice(running[2], stat_blk, (0, 0, row_first, 0))
        updated = (attended, query_grad, stats)
        grad_corner = (0, 0, row_first, 0, 0)
        region = lax.dynamic_slice(running[3], grad_corner, (2, HEADS, 16, padded_cols, depth))
        region = region + results[4].reshape(2, HEADS, 16, padded_cols, depth)
        updated = updated + (lax.dynamic_update_slice(running[3], region, grad_corner),)
        return updated

    finished = lax.fori_loop(0, block_count, query_step, initial)
    key_grad, value_grad = return_rims(finished[3], tile_rows, tile_cols)
    return (from_heads(finished[0]), from_heads(finished[1]), key_grad, value_grad)


def solution(mesh):
    placed = (
        P(("region", "row"), "col", None),
        P(("region", "row"), "col", None),
        P(("region", "row"), "col", None),
        P(("region", "row"), "col", None),
        P("region", None),
        P("region", None),
    )
    return jax.shard_map(
        local,
        mesh=mesh,
        in_specs=placed,
        out_specs=(
            P(("region", "row"), "col", None),
            P(("region", "row"), "col", None),
            P(("region", "row"), "col", None),
            P(("region", "row"), "col", None),
        ),
        check_vma=False,
    )
```

profile of v0, /device:TPU:1, one launch (start us, length us, event | category | flops | bytes accessed | tf_op | source)
XLA Modules:
  0.0 185.5 jit_solution(4608292675208341406)
XLA Ops:
  4.1 4.5 %collective-permute-start = (bf16[2,12,4,8,64]{4,1,3,2,0:T(8,128)(2,1)S(1)}, bf16[2,12,4,8,64]{4,1,3,2,0:T(8,128)(2,1)S(1)}, u32[]{:S(2)}, u32[]{:S(2)}) collective-permute-start(bf16[2,12,4,8,64]{4,1,3,2,0:T(8,128)(2,1)S(1)} %get-tuple-element.410), channel_id=1, source_target_pairs={{0,4},{4,8},{8,12},{1,5},{5,9},{9,13},{2,6},{6,10},{10,14},{3,7},{... | collective-permute-start | bytes 294920 | tf_op jit(solution)/shard_map/ppermute | solution.py:25
  11.9 4.4 %collective-permute-done.1 = bf16[2,12,4,8,64]{4,1,3,2,0:T(8,128)(2,1)S(1)} collective-permute-done((bf16[2,12,4,8,64]{4,1,3,2,0:T(8,128)(2,1)S(1)}, bf16[2,12,4,8,64]{4,1,3,2,0:T(8,128)(2,1)S(1)}, u32[]{:S(2)}, u32[]{:S(2)}) %collective-permute-start.1) | collective-permute-done | bytes 98336 | tf_op jit(solution)/shard_map/ppermute | solution.py:26
  22.4 4.9 %collective-permute-start.2 = (bf16[2,12,40,4,64]{4,2,3,1,0:T(8,128)(2,1)}, bf16[2,12,40,4,64]{4,2,3,1,0:T(8,128)(2,1)}, u32[]{:S(2)}, u32[]{:S(2)}) collective-permute-start(bf16[2,12,40,4,64]{4,2,3,1,0:T(8,128)(2,1)} %copy.63), channel_id=1, source_target_pairs={{0,1},{1,2},{2,3},{4,5},{5,6},{6,7},{8,9},{9,10},{10,11},{12,13},{... | collective-permute-start | bytes 1474568 | tf_op jit(solution)/shard_map/ppermute | solution.py:25
  30.9 2.5 %reshape.409 = bf16[32,8,12,64]{3,2,1,0:T(8,128)(2,1)} reshape(bf16[32,8,768]{2,1,0:T(8,128)(2,1)} %param.21) | data formatting | bytes 786432 | tf_op jit(solution)/shard_map/reshape | solution.py:53
  34.8 8.2 %collective-permute-done.3 = bf16[2,12,40,4,64]{4,2,3,1,0:T(8,128)(2,1)} collective-permute-done((bf16[2,12,40,4,64]{4,2,3,1,0:T(8,128)(2,1)}, bf16[2,12,40,4,64]{4,2,3,1,0:T(8,128)(2,1)}, u32[]{:S(2)}, u32[]{:S(2)}) %collective-permute-start.3) | collective-permute-done | bytes 491552 | tf_op jit(solution)/shard_map/ppermute | solution.py:26
  46.4 6.4 %pad_maximum_fusion = bf16[2,12,40,16,64]{4,1,3,2,0:T(8,128)(2,1)S(1)} fusion(bf16[2,12,40,4,64]{4,1,3,2,0:T(8,128)(2,1)S(1)} %copy.66, bf16[2,12,4,8,64]{4,1,3,2,0:T(8,128)(2,1)S(1)} %copy-done.5, bf16[1,12,32,8,64]{4,1,3,2,0:T(8,128)(2,1)S(1)} %bitcast.102, bf16[1,12,32,8,64]{4,1,3,2,0:T(8,128)(2,1)S(1)} %bitcast.99, ...), kind=kLoop, calls=%fused_computation.42 | loop fusion | flops 4915200 | bytes 3932160 | tf_op jit(solution)/shard_map/concatenate | solution.py:27
  53.8 3.7 %pad.21.clone = bf16[2,12,40,24,64]{4,3,2,1,0:T(8,128)(2,1)} pad(bf16[2,12,40,16,64]{4,3,2,1,0:T(8,128)(2,1)S(1)} %copy.89, bf16[]{:T(256)} %constant.239.clone.1), padding=0_0x0_0x0_0x0_8x0_0 | pad | bytes 4915202 | tf_op jit(solution)/shard_map/jit(_pad)/pad | solution.py:65
  59.6 5.7 %broadcast_in_dim.68 = f32[2,12,40,24,64]{4,3,2,1,0:T(8,128)} broadcast(f32[]{:T(128)} %constant.240.clone.1), dimensions={} | broadcast | bytes 5898244 | tf_op jit(solution)/shard_map/broadcast_in_dim | solution.py:191
  65.3 55.8 %while.24 = (s32[]{:T(128)}, bf16[12,32,8,64]{3,2,1,0:T(8,128)(2,1)}, bf16[12,32,8,64]{3,2,1,0:T(8,128)(2,1)}, f32[2,12,40,24,64]{4,3,2,1,0:T(8,128)}, s32[40,24...) while((s32[]{:T(128)}, ...), condition=%wide.region_3.4_spmd.clone, body=%wide.region_0.3_spmd.sunk.clone.sunk | while | flops 233397200 | bytes 90796744 | solution.py:212
  66.2 2.2 %constant_dynamic-slice_fusion.7 = (bf16[1,12,16,24,64]{4,3,2,1,0:T(8,128)(2,1)S(1)}, bf16[1,12,16,24,64]{4,3,2,1,0:T(8,128)(2,1)S(1)}) fusion(bf16[2,12,40,24,64]{4,3,2,1,0:T(8,128)(2,1)} %get-tuple-element.528, s32[]{:T(128)S(6)} %select_n.128, s32[]{:T(128)S(6)} %add.193), kind=kLoop, calls=%fused_computation.34.clone.1 | loop fusion | bytes 2359304 | tf_op jit(solution)/shard_map/while/body/eval_jaxpr/slice | solution.py:108
  75.1 4.3 %copy-done = f32[2,12,40,24,64]{4,3,2,1,0:T(8,128)} copy-done((f32[2,12,40,24,64]{4,3,2,1,0:T(8,128)}, f32[2,12,40,24,64]{4,3,2,1,0:T(8,128)S(1)}, u32[]{:S(2)}) %copy-start) | copy-done | bytes 5898264 | tf_op jit(solution)/shard_map/while
  80.1 2.2 %constant_dynamic-slice_fusion.7 = (bf16[1,12,16,24,64]{4,3,2,1,0:T(8,128)(2,1)S(1)}, bf16[1,12,16,24,64]{4,3,2,1,0:T(8,128)(2,1)S(1)}) fusion(bf16[2,12,40,24,64]{4,3,2,1,0:T(8,128)(2,1)} %get-tuple-element.528, s32[]{:T(128)S(6)} %select_n.128, s32[]{:T(128)S(6)} %add.193), kind=kLoop, calls=%fused_computation.34.clone.1 | loop fusion | bytes 2359304 | tf_op jit(solution)/shard_map/while/body/eval_jaxpr/slice | solution.py:108
  89.0 4.3 %copy-done = f32[2,12,40,24,64]{4,3,2,1,0:T(8,128)} copy-done((f32[2,12,40,24,64]{4,3,2,1,0:T(8,128)}, f32[2,12,40,24,64]{4,3,2,1,0:T(8,128)S(1)}, u32[]{:S(2)}) %copy-start) | copy-done | bytes 5898264 | tf_op jit(solution)/shard_map/while
  102.9 4.3 %copy-done = f32[2,12,40,24,64]{4,3,2,1,0:T(8,128)} copy-done((f32[2,12,40,24,64]{4,3,2,1,0:T(8,128)}, f32[2,12,40,24,64]{4,3,2,1,0:T(8,128)S(1)}, u32[]{:S(2)}) %copy-start) | copy-done | bytes 5898264 | tf_op jit(solution)/shard_map/while
  116.8 4.3 %copy-done = f32[2,12,40,24,64]{4,3,2,1,0:T(8,128)} copy-done((f32[2,12,40,24,64]{4,3,2,1,0:T(8,128)}, f32[2,12,40,24,64]{4,3,2,1,0:T(8,128)S(1)}, u32[]{:S(2)}) %copy-start) | copy-done | bytes 5898264 | tf_op jit(solution)/shard_map/while
  121.1 5.3 %convert.12 = bf16[2,12,40,24,64]{4,3,2,1,0:T(8,128)(2,1)S(1)} convert(f32[2,12,40,24,64]{4,3,2,1,0:T(8,128)} %get-tuple-element.320) | non-fusion elementwise | flops 1474560 | bytes 8847360 | tf_op jit(solution)/shard_map/convert.5
  128.5 4.5 %collective-permute-start.5 = (bf16[2,12,40,4,64]{4,3,2,1,0:T(4,128)(2,1)S(1)}, bf16[2,12,40,4,64]{4,3,2,1,0:T(4,128)(2,1)S(1)}, u32[]{:S(2)}, u32[]{:S(2)}) collective-permute-start(bf16[2,12,40,4,64]{4,3,2,1,0:T(4,128)(2,1)S(1)} %get-tuple-element.406), channel_id=1, source_target_pairs={{0,1},{1,2},{2,3},{4,5},{5,6},{6,7},{8,9},{9,10},{10,11},{12,13},{... | collective-permute-start | bytes 1474568 | tf_op jit(solution)/shard_map/ppermute | solution.py:15
  133.0 17.3 %collective-permute-done.4 = bf16[2,12,40,4,64]{4,3,2,1,0:T(4,128)(2,1)S(1)} collective-permute-done((bf16[2,12,40,4,64]{4,3,2,1,0:T(4,128)(2,1)S(1)}, bf16[2,12,40,4,64]{4,3,2,1,0:T(4,128)(2,1)S(1)}, u32[]{:S(2)}, u32[]{:S(2)}) %collective-permute-start.4) | collective-permute-done | bytes 491552 | tf_op jit(solution)/shard_map/ppermute | solution.py:15
  150.3 4.1 %add_dynamic-update-slice_fusion = f32[2,12,40,24,64]{4,3,2,1,0:T(8,128)} fusion(f32[2,12,40,24,64]{4,3,2,1,0:T(8,128)} %get-tuple-element.320, bf16[2,12,40,4,64]{4,3,2,1,0:T(4,128)(2,1)S(1)} %collective-permute-done.4), kind=kLoop, calls=%fused_computation.46 | loop fusion | flops 491520 | bytes 4423680 | tf_op jit(solution)/shard_map/scatter-add | solution.py:144
  154.5 4.3 %fusion.26 = f32[2,12,40,24,64]{4,3,2,1,0:T(8,128)} fusion(f32[2,12,40,24,64]{4,3,2,1,0:T(8,128)} %add_dynamic-update-slice_fusion, bf16[2,12,40,4,64]{4,3,2,1,0:T(4,128)(2,1)S(1)} %collective-permute-done.5), kind=kLoop, calls=%fused_computation.45 | loop fusion | flops 491520 | bytes 4423680 | tf_op jit(solution)/shard_map/scatter-add | solution.py:145
  158.8 5.4 %convert.13 = bf16[2,12,40,24,64]{4,3,2,1,0:T(8,128)(2,1)S(1)} convert(f32[2,12,40,24,64]{4,3,2,1,0:T(8,128)} %fusion.26) | non-fusion elementwise | flops 1474560 | bytes 8847360 | tf_op jit(solution)/shard_map/convert.3
  164.4 2.3 %collective-permute-start.6 = (bf16[2,12,4,8,64]{4,3,2,1,0:T(8,128)(2,1)S(1)}, bf16[2,12,4,8,64]{4,3,2,1,0:T(8,128)(2,1)S(1)}, u32[]{:S(2)}, u32[]{:S(2)}) collective-permute-start(bf16[2,12,4,8,64]{4,3,2,1,0:T(8,128)(2,1)S(1)} %get-tuple-element.405), channel_id=1, source_target_pairs={{4,0},{8,4},{12,8},{5,1},{9,5},{13,9},{6,2},{10,6},{14,10},{7,3},{... | collective-permute-start | bytes 294920 | tf_op jit(solution)/shard_map/ppermute | solution.py:15
  171.1 3.3 %slice.230 = f32[2,12,32,8,64]{4,3,2,1,0:T(8,128)S(1)} slice(f32[2,12,40,24,64]{4,3,2,1,0:T(8,128)} %fusion.26), slice={[0:2], [0:12], [4:36], [4:12], [0:64]} | slice | bytes 3145728 | tf_op jit(solution)/shard_map/slice | solution.py:154
  174.4 3.6 %collective-permute-start.7 = (bf16[2,12,4,8,64]{4,3,2,1,0:T(8,128)(2,1)S(1)}, bf16[2,12,4,8,64]{4,3,2,1,0:T(8,128)(2,1)S(1)}, u32[]{:S(2)}, u32[]{:S(2)}) collective-permute-start(bf16[2,12,4,8,64]{4,3,2,1,0:T(8,128)(2,1)S(1)} %get-tuple-element.404), channel_id=1, source_target_pairs={{0,4},{4,8},{8,12},{1,5},{5,9},{9,13},{2,6},{6,10},{10,14},{3,7},{... | collective-permute-start | bytes 294920 | tf_op jit(solution)/shard_map/ppermute | solution.py:15
  (176 shorter events, 71.5 us)
Async XLA Ops:
  4.1 7.8 %collective-permute-start = (bf16[2,12,4,8,64]{4,1,3,2,0:T(8,128)(2,1)S(1)}, bf16[2,12,4,8,64]{4,1,3,2,0:T(8,128)(2,1)S(1)}, u32[]{:S(2)}, u32[]{:S(2)}) collective-permute-start(bf16[2,12,4,8,64]{4,1,3,2,0:T(8,128)(2,1)S(1)} %get-tuple-element.410), channel_id=1, source_target_pairs={{0,4},{4,8},{8,12},{1,5},{5,9},{9,13},{2,6},{6,10},{10,14},{3,7},{... | collective-permute-start | bytes 294920 | tf_op jit(solution)/shard_map/ppermute | solution.py:25
  8.7 7.7 %collective-permute-start.1 = (bf16[2,12,4,8,64]{4,1,3,2,0:T(8,128)(2,1)S(1)}, bf16[2,12,4,8,64]{4,1,3,2,0:T(8,128)(2,1)S(1)}, u32[]{:S(2)}, u32[]{:S(2)}) collective-permute-start(bf16[2,12,4,8,64]{4,1,3,2,0:T(8,128)(2,1)S(1)} %get-tuple-element.411), channel_id=1, source_target_pairs={{4,0},{8,4},{12,8},{5,1},{9,5},{13,9},{6,2},{10,6},{14,10},{7,3},{... | collective-permute-start | bytes 294920 | tf_op jit(solution)/shard_map/ppermute | solution.py:26
  17.9 9.5 %copy-start.8 = (s32[16,4]{0,1:T(4,128)S(1)}, s32[16,4]{0,1:T(4,128)}, u32[]{:S(2)}) copy-start(s32[16,4]{0,1:T(4,128)} %param.23) | copy-start | bytes 772
  17.9 9.4 %copy-start.9 = (s32[16,4]{0,1:T(4,128)S(1)}, s32[16,4]{0,1:T(4,128)}, u32[]{:S(2)}) copy-start(s32[16,4]{0,1:T(4,128)} %param.22) | copy-start | bytes 772
  21.2 21.9 %collective-permute-start.3 = (bf16[2,12,40,4,64]{4,2,3,1,0:T(8,128)(2,1)}, bf16[2,12,40,4,64]{4,2,3,1,0:T(8,128)(2,1)}, u32[]{:S(2)}, u32[]{:S(2)}) collective-permute-start(bf16[2,12,40,4,64]{4,2,3,1,0:T(8,128)(2,1)} %copy.64), channel_id=1, source_target_pairs={{1,0},{2,1},{3,2},{5,4},{6,5},{7,6},{9,8},{10,9},{11,10},{13,12},{... | collective-permute-start | bytes 1474568 | tf_op jit(solution)/shard_map/ppermute | solution.py:26
  22.4 22.4 %collective-permute-start.2 = (bf16[2,12,40,4,64]{4,2,3,1,0:T(8,128)(2,1)}, bf16[2,12,40,4,64]{4,2,3,1,0:T(8,128)(2,1)}, u32[]{:S(2)}, u32[]{:S(2)}) collective-permute-start(bf16[2,12,40,4,64]{4,2,3,1,0:T(8,128)(2,1)} %copy.63), channel_id=1, source_target_pairs={{0,1},{1,2},{2,3},{4,5},{5,6},{6,7},{8,9},{9,10},{10,11},{12,13},{... | collective-permute-start | bytes 1474568 | tf_op jit(solution)/shard_map/ppermute | solution.py:25
  34.8 11.6 %copy-start.5 = (bf16[2,12,4,8,64]{4,1,3,2,0:T(8,128)(2,1)S(1)}, bf16[2,12,4,8,64]{4,1,3,2,0:T(8,128)(2,1)}, u32[]{:S(2)}) copy-start(bf16[2,12,4,8,64]{4,1,3,2,0:T(8,128)(2,1)} %copy-done.4) | copy-start | bytes 294916
  59.6 5.7 %copy-start.1 = (bf16[12,32,8,64]{3,2,1,0:T(8,128)(2,1)S(1)}, bf16[12,32,8,64]{3,2,1,0:T(8,128)(2,1)}, u32[]{:S(2)}) copy-start(bf16[12,32,8,64]{3,2,1,0:T(8,128)(2,1)} %copy.69) | copy-start | bytes 1179652
  59.6 5.7 %copy-start.6 = (pred[64,384]{1,0:T(32,128)(4,1)S(1)}, pred[64,384]{1,0:T(32,128)(4,1)}, u32[]{:S(2)}) copy-start(pred[64,384]{1,0:T(32,128)(4,1)} %constant.252.clone..sunk.2) | copy-start | bytes 73732
  59.6 5.7 %copy-start.7 = (pred[64,384]{1,0:T(32,128)(4,1)S(1)}, pred[64,384]{1,0:T(32,128)(4,1)}, u32[]{:S(2)}) copy-start(pred[64,384]{1,0:T(32,128)(4,1)} %constant.253.clone..sunk.2) | copy-start | bytes 73732
  66.2 7.8 %slice-start = ((s8[11796480]{0:T(1024)(128)(4,1)}), s8[4194304]{0:T(1024)(128)(4,1)S(1)}, s32[]{:S(2)}) async-start(s8[11796480]{0:T(1024)(128)(4,1)} %bitcast.89), calls=%async_computation | async-start | bytes 8388608 | tf_op jit(solution)/shard_map/while
  69.1 4.9 %slice-start.1 = ((s8[11796480]{0:T(1024)(128)(4,1)}), s8[4194304]{0:T(1024)(128)(4,1)S(1)}, s32[]{:S(2)}) async-start(s8[11796480]{0:T(1024)(128)(4,1)} %bitcast.89), calls=%async_computation.1 | async-start | bytes 8388608 | tf_op jit(solution)/shard_map/while
  80.1 7.8 %slice-start = ((s8[11796480]{0:T(1024)(128)(4,1)}), s8[4194304]{0:T(1024)(128)(4,1)S(1)}, s32[]{:S(2)}) async-start(s8[11796480]{0:T(1024)(128)(4,1)} %bitcast.89), calls=%async_computation | async-start | bytes 8388608 | tf_op jit(solution)/shard_map/while
  83.1 4.9 %slice-start.1 = ((s8[11796480]{0:T(1024)(128)(4,1)}), s8[4194304]{0:T(1024)(128)(4,1)S(1)}, s32[]{:S(2)}) async-start(s8[11796480]{0:T(1024)(128)(4,1)} %bitcast.89), calls=%async_computation.1 | async-start | bytes 8388608 | tf_op jit(solution)/shard_map/while
  94.0 7.8 %slice-start = ((s8[11796480]{0:T(1024)(128)(4,1)}), s8[4194304]{0:T(1024)(128)(4,1)S(1)}, s32[]{:S(2)}) async-start(s8[11796480]{0:T(1024)(128)(4,1)} %bitcast.89), calls=%async_computation | async-start | bytes 8388608 | tf_op jit(solution)/shard_map/while
  97.0 4.8 %slice-start.1 = ((s8[11796480]{0:T(1024)(128)(4,1)}), s8[4194304]{0:T(1024)(128)(4,1)S(1)}, s32[]{:S(2)}) async-start(s8[11796480]{0:T(1024)(128)(4,1)} %bitcast.89), calls=%async_computation.1 | async-start | bytes 8388608 | tf_op jit(solution)/shard_map/while
  107.9 7.8 %slice-start = ((s8[11796480]{0:T(1024)(128)(4,1)}), s8[4194304]{0:T(1024)(128)(4,1)S(1)}, s32[]{:S(2)}) async-start(s8[11796480]{0:T(1024)(128)(4,1)} %bitcast.89), calls=%async_computation | async-start | bytes 8388608 | tf_op jit(solution)/shard_map/while
  110.8 4.8 %slice-start.1 = ((s8[11796480]{0:T(1024)(128)(4,1)}), s8[4194304]{0:T(1024)(128)(4,1)S(1)}, s32[]{:S(2)}) async-start(s8[11796480]{0:T(1024)(128)(4,1)} %bitcast.89), calls=%async_computation.1 | async-start | bytes 8388608 | tf_op jit(solution)/shard_map/while
  127.2 23.1 %collective-permute-start.4 = (bf16[2,12,40,4,64]{4,3,2,1,0:T(4,128)(2,1)S(1)}, bf16[2,12,40,4,64]{4,3,2,1,0:T(4,128)(2,1)S(1)}, u32[]{:S(2)}, u32[]{:S(2)}) collective-permute-start(bf16[2,12,40,4,64]{4,3,2,1,0:T(4,128)(2,1)S(1)} %get-tuple-element.407), channel_id=1, source_target_pairs={{1,0},{2,1},{3,2},{5,4},{6,5},{7,6},{9,8},{10,9},{11,10},{13,12},{... | collective-permute-start | bytes 1474568 | tf_op jit(solution)/shard_map/ppermute | solution.py:15
  128.5 26.0 %collective-permute-start.5 = (bf16[2,12,40,4,64]{4,3,2,1,0:T(4,128)(2,1)S(1)}, bf16[2,12,40,4,64]{4,3,2,1,0:T(4,128)(2,1)S(1)}, u32[]{:S(2)}, u32[]{:S(2)}) collective-permute-start(bf16[2,12,40,4,64]{4,3,2,1,0:T(4,128)(2,1)S(1)} %get-tuple-element.406), channel_id=1, source_target_pairs={{0,1},{1,2},{2,3},{4,5},{5,6},{6,7},{8,9},{9,10},{10,11},{12,13},{... | collective-permute-start | bytes 1474568 | tf_op jit(solution)/shard_map/ppermute | solution.py:15
  158.8 7.9 %copy-start.2 = (bf16[12,32,8,64]{3,2,1,0:T(8,128)(2,1)S(1)}, bf16[12,32,8,64]{3,2,1,0:T(8,128)(2,1)}, u32[]{:S(2)}) copy-start(bf16[12,32,8,64]{3,2,1,0:T(8,128)(2,1)} %get-tuple-element.319) | copy-start | bytes 1179652
  164.2 4.7 %copy-start.3 = (bf16[12,32,8,64]{3,2,1,0:T(8,128)(2,1)S(1)}, bf16[12,32,8,64]{3,2,1,0:T(8,128)(2,1)}, u32[]{:S(2)}) copy-start(bf16[12,32,8,64]{3,2,1,0:T(8,128)(2,1)} %get-tuple-element.318) | copy-start | bytes 1179652
  164.4 13.6 %collective-permute-start.6 = (bf16[2,12,4,8,64]{4,3,2,1,0:T(8,128)(2,1)S(1)}, bf16[2,12,4,8,64]{4,3,2,1,0:T(8,128)(2,1)S(1)}, u32[]{:S(2)}, u32[]{:S(2)}) collective-permute-start(bf16[2,12,4,8,64]{4,3,2,1,0:T(8,128)(2,1)S(1)} %get-tuple-element.405), channel_id=1, source_target_pairs={{4,0},{8,4},{12,8},{5,1},{9,5},{13,9},{6,2},{10,6},{14,10},{7,3},{... | collective-permute-start | bytes 294920 | tf_op jit(solution)/shard_map/ppermute | solution.py:15
  174.4 6.2 %collective-permute-start.7 = (bf16[2,12,4,8,64]{4,3,2,1,0:T(8,128)(2,1)S(1)}, bf16[2,12,4,8,64]{4,3,2,1,0:T(8,128)(2,1)S(1)}, u32[]{:S(2)}, u32[]{:S(2)}) collective-permute-start(bf16[2,12,4,8,64]{4,3,2,1,0:T(8,128)(2,1)S(1)} %get-tuple-element.404), channel_id=1, source_target_pairs={{0,4},{4,8},{8,12},{1,5},{5,9},{9,13},{2,6},{6,10},{10,14},{3,7},{... | collective-permute-start | bytes 294920 | tf_op jit(solution)/shard_map/ppermute | solution.py:15
  (9 other events, 28.0 us)
where the time goes:
time: 187 us; the launch traced here: 185 us
  local copies, waits for them, and re-layouts  71.4 us (38%)
  other arithmetic  35.4 us (19%)
  waiting for transfers between devices  32.8 us (18%)
  starting transfers between devices  24.4 us (13%)
  matrix products  19.8 us (11%)
    ppermute x4, waiting for transfers between devices, shifted(): return lax.ppermute(block, axis, route)  18.7 us
    while x32, local copies, waits for them, and re-layouts  17.4 us
    ppermute x2, waiting for transfers between devices, extended_2(): after = lax.ppermute(leading, axis, down)  12.6 us
    ppermute x4, starting transfers between devices, shifted(): return lax.ppermute(block, axis, route)  11.7 us
    another operation x3, other arithmetic  11.1 us
    ppermute x2, starting transfers between devices, extended_2(): before = lax.ppermute(last, axis, up)  9.48 us
    slice x4, local copies, waits for them, and re-layouts, query_center(): key_reg = region[0].reshape(heads, 16 * padded_cols, depth)  8.79 us
    reshape x4, local copies, waits for them, and re-layouts, to_heads(): array.reshape(rows, cols, HEADS, feature // HEADS).transpose(2, 0, 1, 3)  7.45 us
  transfers between devices with their start and end apart: 8, of which 6 were waited for; matrix products, arithmetic and copies ran while one was open for 12% of the time, Pallas kernels for 0%

commit v1 on v0

v1 whole, which is shorter than its diff:
```python
import functools

import jax
import jax.numpy as jnp
import numpy as np
from jax import lax
from jax.experimental import pallas as pl
from jax.experimental.pallas import tpu as pltpu
from jax.sharding import PartitionSpec as P

HEADS = 12
LABEL = 8
REACH = 3
RIM = 4
PACK = 16
MESH = pl.DeviceIdType.MESH
BF16 = jnp.bfloat16
F32 = jnp.float32


def edge_places(rows):
    places = [None] * (2 * PACK + REACH * rows)
    for t in range(RIM * REACH):
        places[t] = (t // REACH - RIM, t % REACH)
        places[PACK + REACH * rows + t] = (rows + t // REACH, t % REACH)
    for t in range(REACH * rows):
        places[PACK + t] = (t // REACH, t % REACH)
    return places


def strip_start(block, rows):
    return min((LABEL * REACH * block + PACK - RIM * REACH) // PACK * PACK, REACH * rows + 2 * PACK - 64)


def edge_picks(rows, cols):
    places = edge_places(rows)
    picks = np.zeros((2, len(places), rows * cols), np.float32)
    for slot, place in enumerate(places):
        if place is not None:
            row, j = place
            picks[0, slot, (row % rows) * cols + j] = 1
            picks[1, slot, (row % rows) * cols + cols - REACH + j] = 1
    return picks.reshape(2 * len(places), rows * cols)


def pair_codes(rows, cols):
    places = edge_places(rows)
    blocks = rows // LABEL
    codes = np.full((blocks, LABEL * cols, 128 + 128), -1, np.float32)
    for b in range(blocks):
        keys = [((LABEL * cols * b + s) // cols - RIM, s % cols) for s in range(128)]
        first = strip_start(b, rows)
        for shift in (-REACH, cols):
            for s in range(64):
                place = places[first + s]
                keys.append(None if place is None else (place[0], place[1] + shift))
        for q in range(LABEL * cols):
            row, col = LABEL * b + q // cols, q % cols
            for n, key in enumerate(keys):
                if key is None or abs(key[0] - row) > REACH or abs(key[1] - col) > REACH:
                    continue
                if key == (row, col):
                    codes[b, q, n] = 9
                else:
                    codes[b, q, n] = (key[0] // LABEL - b + 1) * 3 + key[1] // LABEL + 1
    return codes


def dot(a, b, contract):
    return lax.dot_general(a, b, ((contract[:1], contract[1:]), ((), ())), preferred_element_type=F32)


def kernel(
    sizes,
    q_ref, k_ref, v_ref, do_ref, tissue_ref, slide_ref, code_ref, pick_ref, place_ref,
    att_ref, dq_ref, dk_ref, dv_ref,
    own, strip, edge, grow, gstrip, rrow, redge, acc, sacc, bias,
    send_sem, recv_sem, gsend_sem, grecv_sem,
):
    rows, cols, groups, width, depth, row_size, col_size = sizes
    tokens = rows * cols
    rim = RIM * cols
    side = REACH * rows
    slots = side + 2 * PACK
    blocks = rows // LABEL
    per_block = LABEL * cols
    stacked = width // depth
    region, row, col = lax.axis_index("region"), lax.axis_index("row"), lax.axis_index("col")

    top, mid, bottom = pl.ds(0, PACK), pl.ds(PACK, side), pl.ds(PACK + side, PACK)
    routes = []
    for source, dc in ((0, -1), (1, 1)):
        routes.append((0, dc, source, mid))
        routes.append((1, dc, source, top))
        routes.append((-1, dc, source, bottom))
    routes.append((-1, 0, 2, None))
    routes.append((1, 0, 3, None))

    def exists(dr, dc):
        good = None
        for at, d, size in ((row, dr, row_size), (col, dc, col_size)):
            if d:
                here = (at + d >= 0) if d < 0 else (at + d < size)
                good = here if good is None else good & here
        return good

    def device(dr, dc):
        return (region, row + dr, col + dc)

    def out_copy(g, n, target):
        dr, dc, source, part = routes[n]
        if source < 2:
            src, dst = edge.at[source, g, :, part], strip.at[1 - source, g, :, part]
        elif source == 2:
            src, dst = own.at[g, :, pl.ds(rim, rim)], own.at[g, :, pl.ds(rim + tokens, rim)]
        else:
            src, dst = own.at[g, :, pl.ds(tokens, rim)], own.at[g, :, pl.ds(0, rim)]
        return pltpu.make_async_remote_copy(
            src_ref=src, dst_ref=dst, send_sem=send_sem.at[g, n], recv_sem=recv_sem.at[g, n],
            device_id=target, device_id_type=MESH)

    def back_copy(g, n, target):
        dr, dc, source, part = routes[n]
        if source < 2:
            src, dst = gstrip.at[1 - source, g, :, part], redge.at[source, g, :, part]
        else:
            src, dst = grow.at[3 - source, g], rrow.at[source - 2, g]
        return pltpu.make_async_remote_copy(
            src_ref=src, dst_ref=dst, send_sem=gsend_sem.at[g, n], recv_sem=grecv_sem.at[g, n],
            device_id=target, device_id_type=MESH)

    zero_rim = jnp.zeros((groups, 2, rim, width), BF16)
    own[:, :, pl.ds(0, rim)] = zero_rim
    own[:, :, pl.ds(rim + tokens, rim)] = zero_rim
    strip[...] = jnp.zeros(strip.shape, BF16)
    redge[...] = jnp.zeros(redge.shape, BF16)
    rrow[...] = jnp.zeros(rrow.shape, BF16)

    barrier = pltpu.get_barrier_semaphore()
    around = jnp.int32(0)
    for dr in (-1, 0, 1):
        for dc in (-1, 0, 1):
            if dr or dc:
                good = exists(dr, dc)
                around = around + good.astype(jnp.int32)

                @pl.when(good)
                def _(dr=dr, dc=dc):
                    pl.semaphore_signal(barrier, inc=1, device_id=device(dr, dc), device_id_type=MESH)

    def stage(g, carry):
        lanes = pl.ds(pl.multiple_of(g * width, width), width)
        for i, ref in enumerate((k_ref, v_ref)):
            block = ref[:, lanes]
            own[g, i, pl.ds(rim, tokens)] = block
            picked = dot(pick_ref[...], block, (1, 0)).astype(BF16)
            edge[0, g, i] = picked[:slots]
            edge[1, g, i] = picked[slots:]
        return carry

    lax.fori_loop(0, groups, stage, 0)
    pl.semaphore_wait(barrier, around)

    def send(g, carry):
        for n, (dr, dc, _, _) in enumerate(routes):
            @pl.when(exists(dr, dc))
            def _(n=n, dr=dr, dc=dc):
                out_copy(g, n, device(dr, dc)).start()
        return carry

    lax.fori_loop(0, groups, send, 0)

    def label(r, c):
        r_all, c_all = tissue_ref.shape
        inside = (r >= 0) & (r < r_all) & (c >= 0) & (c < c_all)
        r, c = jnp.clip(r, 0, r_all - 1), jnp.clip(c, 0, c_all - 1)
        return jnp.where(inside & (tissue_ref[r, c] == 1), slide_ref[r, c] + 1, 0)

    labels = [[label(row * blocks + i - 1, col + j - 1) for j in range(3)] for i in range(blocks + 2)]
    for b in range(blocks):
        code = code_ref[b]
        mine = labels[b + 1][1]
        level = jnp.where(code == 9, 0.0, -1e30)
        for n in range(9):
            value = jnp.where((mine > 0) & (labels[b + n // 3][n % 3] == mine), 0.0, -1e30)
            level = jnp.where(code == n, value, level)
        bias[b] = level

    lane_head = lax.broadcasted_iota(jnp.int32, (per_block, width), 1) // depth

    def stack(block):
        zero = jnp.zeros_like(block)
        return jnp.concatenate([jnp.where(lane_head == h, block, zero) for h in range(stacked)], axis=0)

    def unstack(full):
        result = full[:per_block]
        for h in range(1, stacked):
            result = jnp.where(lane_head == h, full[h * per_block:(h + 1) * per_block], result)
        return result

    def compute(g, carry):
        for n, (dr, dc, _, _) in enumerate(routes):
            @pl.when(exists(-dr, -dc))
            def _(n=n, dr=dr, dc=dc):
                out_copy(g, n, device(-dr, -dc)).wait_recv()
        lanes = pl.ds(pl.multiple_of(g * width, width), width)
        acc[g] = jnp.zeros(acc.shape[1:], F32)
        sacc[...] = jnp.zeros(sacc.shape, F32)
        for b in range(blocks):
            mine = pl.ds(b * per_block, per_block)
            near = pl.ds(b * per_block, 128)
            far = pl.ds(strip_start(b, rows), 64)
            scale = 1.0 / depth ** 0.5
            q = stack((q_ref[mine, lanes].astype(F32) * scale).astype(BF16))
            grad_block = do_ref[mine, lanes]
            do = stack(grad_block)
            keys, values = (
                jnp.concatenate([own[g, i, near], strip[0, g, i, far], strip[1, g, i, far]], axis=0)
                for i in range(2))
            level = bias[b]
            scores = dot(q, keys, (1, 1)) + jnp.concatenate([level] * stacked, axis=0)
            highest = jnp.max(scores, axis=1, keepdims=True)
            powers = jnp.exp(scores - highest)
            total = jnp.sum(powers, axis=1, keepdims=True)
            weights = powers * (1.0 / total)
            soft = weights.astype(BF16)
            attended = unstack(dot(soft, values, (1, 0))).astype(BF16)
            att_ref[mine, lanes] = attended
            product = grad_block.astype(F32) * attended.astype(F32)
            delta = jnp.concatenate(
                [jnp.sum(jnp.where(lane_head == h, product, 0.0), axis=1, keepdims=True) for h in range(stacked)],
                axis=0)
            prob_grad = dot(do, values, (1, 1))
            score_grad = (weights * (prob_grad - delta)).astype(BF16)
            dq_ref[mine, lanes] = (unstack(dot(score_grad, keys, (1, 0))) * scale).astype(BF16)
            for i, part in enumerate((dot(score_grad, q, (0, 0)), dot(soft, do, (0, 0)))):
                acc[g, i, near] += part[:128]
                sacc[0, i, far] += part[128:192]
                sacc[1, i, far] += part[192:]
        grow[0, g] = acc[g, :, pl.ds(0, rim)].astype(BF16)
        grow[1, g] = acc[g, :, pl.ds(rim + tokens, rim)].astype(BF16)
        gstrip[:, g] = sacc[...].astype(BF16)
        for n, (dr, dc, _, _) in enumerate(routes):
            @pl.when(exists(-dr, -dc))
            def _(n=n, dr=dr, dc=dc):
                back_copy(g, n, device(-dr, -dc)).start()
        return carry

    lax.fori_loop(0, groups, compute, 0)

    def finish(g, carry):
        for n, (dr, dc, _, _) in enumerate(routes):
            @pl.when(exists(dr, dc))
            def _(n=n, dr=dr, dc=dc):
                out_copy(g, n, device(dr, dc)).wait_send()
                back_copy(g, n, device(dr, dc)).wait_recv()
        lanes = pl.ds(pl.multiple_of(g * width, width), width)
        for i, ref in enumerate((dk_ref, dv_ref)):
            edges = jnp.concatenate([redge[0, g, i], redge[1, g, i]], axis=0)
            acc[g, i, pl.ds(rim, rim)] += rrow[0, g, i].astype(F32)
            acc[g, i, pl.ds(tokens, rim)] += rrow[1, g, i].astype(F32)
            total = acc[g, i, pl.ds(rim, tokens)] + dot(place_ref[...], edges, (1, 0))
            ref[:, lanes] = total.astype(BF16)
        for n, (dr, dc, _, _) in enumerate(routes):
            @pl.when(exists(-dr, -dc))
            def _(n=n, dr=dr, dc=dc):
                back_copy(g, n, device(-dr, -dc)).wait_send()
        return carry

    lax.fori_loop(0, groups, finish, 0)


def local(queries, key_states, value_states, out_grad, tissue, slide_id):
    rows, cols, feature = queries.shape
    depth = feature // HEADS
    stacked = 4
    width = stacked * depth
    groups = feature // width
    tokens = rows * cols
    rim = RIM * cols
    slots = REACH * rows + 2 * PACK
    sizes = (rows, cols, groups, width, depth, lax.axis_size("row"), lax.axis_size("col"))
    picks = edge_picks(rows, cols)
    flat = [a.reshape(tokens, feature) for a in (queries, key_states, value_states, out_grad)]
    vmem = pl.BlockSpec(memory_space=pltpu.VMEM)
    smem = pl.BlockSpec(memory_space=pltpu.SMEM)
    outs = pl.pallas_call(
        functools.partial(kernel, sizes),
        out_shape=[jax.ShapeDtypeStruct((tokens, feature), BF16)] * 4,
        in_specs=[vmem] * 4 + [smem] * 2 + [vmem] * 3,
        out_specs=[vmem] * 4,
        scratch_shapes=[
            pltpu.VMEM((groups, 2, tokens + 2 * rim, width), BF16),
            pltpu.VMEM((2, groups, 2, slots, width), BF16),
            pltpu.VMEM((2, groups, 2, slots, width), BF16),
            pltpu.VMEM((2, groups, 2, rim, width), BF16),
            pltpu.VMEM((2, groups, 2, slots, width), BF16),
            pltpu.VMEM((2, groups, 2, rim, width), BF16),
            pltpu.VMEM((2, groups, 2, slots, width), BF16),
            pltpu.VMEM((groups, 2, tokens + 2 * rim, width), F32),
            pltpu.VMEM((2, 2, slots, width), F32),
            pltpu.VMEM((rows // LABEL, LABEL * cols, 256), F32),
            pltpu.SemaphoreType.DMA((groups, 8)),
            pltpu.SemaphoreType.DMA((groups, 8)),
            pltpu.SemaphoreType.DMA((groups, 8)),
            pltpu.SemaphoreType.DMA((groups, 8)),
        ],
        compiler_params=pltpu.CompilerParams(
            collective_id=0, has_side_effects=True, vmem_limit_bytes=48 * 2 ** 20),
        name="window_attention",
    )(
        *flat, tissue, slide_id,
        jnp.asarray(pair_codes(rows, cols)),
        jnp.asarray(picks, BF16),
        jnp.asarray(picks.T, BF16),
    )
    return tuple(a.reshape(rows, cols, feature) for a in outs)


def solution(mesh):
    tile = P(("region", "row"), "col", None)
    table = P("region", None)
    return jax.shard_map(
        local,
        mesh=mesh,
        in_specs=(tile,) * 4 + (table,) * 2,
        out_specs=(tile,) * 4,
        check_vma=False,
    )
```

time: 187 us -> 39.1 us (0.21)
  local copies, waits for them, and re-layouts: 71.4 us -> 11.2 us
  other arithmetic: 35.4 us -> 0 us
  waiting for transfers between devices: 32.8 us -> 0 us
  Pallas kernels: 0 us -> 26.6 us
  starting transfers between devices: 24.4 us -> 0 us
  matrix products: 19.8 us -> 0 us
    ppermute x8 -> x0, waiting for transfers between devices: 32.8 us -> none  [the longest x4 18.7 us: shifted(): return lax.ppermute(block, axis, route)]
    pallas_call x0 -> x1, Pallas kernels: none -> 26.6 us  [local(): pl.pallas_call(functools.partial(kernel, sizes), out_shape=[jax.ShapeDtyp...]
    ppermute x8 -> x0, starting transfers between devices: 24.4 us -> none  [the longest x4 11.7 us: shifted(): return lax.ppermute(block, axis, route)]
    dot_general x24 -> x0, matrix products: 19.8 us -> none  [the longest x4 4.62 us: query_center(): jnp.einsum('hqk,hkd->hqd', soft_weights, value_reg, preferred_element_typ...]
    while x32 -> x0, local copies, waits for them, and re-layouts: 17.4 us -> none
    slice x12 -> x0, local copies, waits for them, and re-layouts: 17 us -> none  [the longest x4 8.79 us: query_center(): key_reg = region[0].reshape(heads, 16 * padded_cols, depth)]
    another operation x3 -> x0, other arithmetic: 11.1 us -> none
    reshape x10 -> x0, local copies, waits for them, and re-layouts: 10.4 us -> none  [the longest x4 7.45 us: to_heads(): array.reshape(rows, cols, HEADS, feature // HEADS).transpose(2, 0, 1, 3)]
  transfers between devices with their start and end apart: 8 -> 0, of which waited for: 6 -> 0; matrix products, arithmetic and copies ran while one was open for 12% -> 0% of each run, Pallas kernels for 0% -> 0%
where the time goes in v1:
time: 39.1 us; the launch traced here: 38.4 us
  Pallas kernels  26.6 us (68%)
  local copies, waits for them, and re-layouts  11.2 us (29%)
  between operations  0.66 us (2%)
    pallas_call x1, Pallas kernels, local(): pl.pallas_call(functools.partial(kernel, sizes), out_shape=[jax.ShapeDtyp...  26.6 us
    unnamed x24, local copies, waits for them, and re-layouts  11.2 us

profile of v1, /device:TPU:1, one launch (start us, length us, event | category | flops | bytes accessed | tf_op | source)
XLA Modules:
  0.0 38.4 jit_solution(4405109097617125869)
XLA Ops:
  0.6 0.0 copy-start.7
  0.6 0.7 %copy-done.7 = s32[16,4]{0,1:T(4,128)S(1)} copy-done((s32[16,4]{0,1:T(4,128)S(1)}, s32[16,4]{0,1:T(4,128)}, u32[]{:S(2)}) %copy-start.7) | copy-done | bytes 280
  1.3 0.0 copy-start.8
  1.3 0.1 copy.13.tissue_ref
  1.4 0.6 %copy-done.8 = s32[16,4]{0,1:T(4,128)S(1)} copy-done((s32[16,4]{0,1:T(4,128)S(1)}, s32[16,4]{0,1:T(4,128)}, u32[]{:S(2)}) %copy-start.8) | copy-done | bytes 280
  2.0 0.1 copy.14.slide_ref
  2.1 0.0 copy-start
  2.1 1.0 %copy-done = bf16[32,8,768]{2,1,0:T(8,128)(2,1)S(1)} copy-done((bf16[32,8,768]{2,1,0:T(8,128)(2,1)S(1)}, bf16[32,8,768]{2,1,0:T(8,128)(2,1)}, u32[]{:S(2)}) %copy-start) | copy-done | bytes 393240
  3.1 0.0 copy-start.1
  3.1 1.0 %copy-done.1 = bf16[32,8,768]{2,1,0:T(8,128)(2,1)S(1)} copy-done((bf16[32,8,768]{2,1,0:T(8,128)(2,1)S(1)}, bf16[32,8,768]{2,1,0:T(8,128)(2,1)}, u32[]{:S(2)}) %copy-start.1) | copy-done | bytes 393240
  4.1 0.0 copy-start.2
  4.1 1.0 %copy-done.2 = bf16[32,8,768]{2,1,0:T(8,128)(2,1)S(1)} copy-done((bf16[32,8,768]{2,1,0:T(8,128)(2,1)S(1)}, bf16[32,8,768]{2,1,0:T(8,128)(2,1)}, u32[]{:S(2)}) %copy-start.2) | copy-done | bytes 393240
  5.1 0.0 copy-start.3
  5.1 1.0 %copy-done.3 = bf16[32,8,768]{2,1,0:T(8,128)(2,1)S(1)} copy-done((bf16[32,8,768]{2,1,0:T(8,128)(2,1)S(1)}, bf16[32,8,768]{2,1,0:T(8,128)(2,1)}, u32[]{:S(2)}) %copy-start.3) | copy-done | bytes 393240
  6.1 0.9 %copy-done.4 = f32[4,64,256]{2,1,0:T(8,128)S(1)} copy-done((f32[4,64,256]{2,1,0:T(8,128)S(1)}, f32[4,64,256]{2,1,0:T(8,128)}, u32[]{:S(2)}) %copy-start.4) | copy-done | bytes 262168
  7.0 0.0 copy-start.5
  7.0 0.9 %copy-done.5 = bf16[256,256]{1,0:T(8,128)(2,1)S(1)} copy-done((bf16[256,256]{1,0:T(8,128)(2,1)S(1)}, bf16[256,256]{1,0:T(8,128)(2,1)}, u32[]{:S(2)}) %copy-start.5) | copy-done | bytes 131096
  7.9 0.0 copy-start.6
  7.9 0.9 %copy-done.6 = bf16[256,256]{1,0:T(8,128)(2,1)S(1)} copy-done((bf16[256,256]{1,0:T(8,128)(2,1)S(1)}, bf16[256,256]{1,0:T(8,128)(2,1)}, u32[]{:S(2)}) %copy-start.6) | copy-done | bytes 131096
  8.8 26.6 %window_attention.1 = (bf16[256,768]{1,0:T(8,128)(2,1)S(1)}, bf16[256,768]{1,0:T(8,128)(2,1)S(1)}, bf16[256,768]{1,0:T(8,128)(2,1)S(1)}, bf16[256,768]{1,0:T(8,128)(2,1)S(1)}) custom-call(bf16[256,768]{1,0:T(8,128)(2,1)S(1)} %bitcast.8, bf16[256,768]{1,0:T(8,128)(2,1)S(1)} %bitcast.9, bf16[256,768]{1,0:T(8,128)(2,1)S(1)} %bitcast.10, ...), custom_call_target="tpu_custom_call" | custom-call | tf_op jit(solution)/shard_map/window_attention/pallas_call | solution.py:287
  35.4 0.7 %copy.19 = bf16[32,8,768]{2,1,0:T(8,128)(2,1)} copy(bf16[32,8,768]{2,1,0:T(8,128)(2,1)S(1)} %bitcast.15) | data formatting | bytes 786432
  36.1 0.7 %copy.20 = bf16[32,8,768]{2,1,0:T(8,128)(2,1)} copy(bf16[32,8,768]{2,1,0:T(8,128)(2,1)S(1)} %bitcast.14) | data formatting | bytes 786432
  36.9 0.7 %copy.21 = bf16[32,8,768]{2,1,0:T(8,128)(2,1)} copy(bf16[32,8,768]{2,1,0:T(8,128)(2,1)S(1)} %bitcast.13) | data formatting | bytes 786432
  37.6 0.7 %copy.22 = bf16[32,8,768]{2,1,0:T(8,128)(2,1)} copy(bf16[32,8,768]{2,1,0:T(8,128)(2,1)S(1)} %bitcast.12) | data formatting | bytes 786432
  (1 shorter events, 0.0 us)
Async XLA Ops:
  0.6 0.7 %copy-start.7 = (s32[16,4]{0,1:T(4,128)S(1)}, s32[16,4]{0,1:T(4,128)}, u32[]{:S(2)}) copy-start(s32[16,4]{0,1:T(4,128)} %param.13) | copy-start | bytes 772
  1.3 0.7 %copy-start.8 = (s32[16,4]{0,1:T(4,128)S(1)}, s32[16,4]{0,1:T(4,128)}, u32[]{:S(2)}) copy-start(s32[16,4]{0,1:T(4,128)} %param.14) | copy-start | bytes 772
  2.1 1.0 %copy-start = (bf16[32,8,768]{2,1,0:T(8,128)(2,1)S(1)}, bf16[32,8,768]{2,1,0:T(8,128)(2,1)}, u32[]{:S(2)}) copy-start(bf16[32,8,768]{2,1,0:T(8,128)(2,1)} %param.9) | copy-start | bytes 1179652
  3.1 1.0 %copy-start.1 = (bf16[32,8,768]{2,1,0:T(8,128)(2,1)S(1)}, bf16[32,8,768]{2,1,0:T(8,128)(2,1)}, u32[]{:S(2)}) copy-start(bf16[32,8,768]{2,1,0:T(8,128)(2,1)} %param.10) | copy-start | bytes 1179652
  4.1 1.0 %copy-start.2 = (bf16[32,8,768]{2,1,0:T(8,128)(2,1)S(1)}, bf16[32,8,768]{2,1,0:T(8,128)(2,1)}, u32[]{:S(2)}) copy-start(bf16[32,8,768]{2,1,0:T(8,128)(2,1)} %param.11) | copy-start | bytes 1179652
  5.1 1.0 %copy-start.3 = (bf16[32,8,768]{2,1,0:T(8,128)(2,1)S(1)}, bf16[32,8,768]{2,1,0:T(8,128)(2,1)}, u32[]{:S(2)}) copy-start(bf16[32,8,768]{2,1,0:T(8,128)(2,1)} %param.12) | copy-start | bytes 1179652
  6.1 0.9 %copy-start.4 = (f32[4,64,256]{2,1,0:T(8,128)S(1)}, f32[4,64,256]{2,1,0:T(8,128)}, u32[]{:S(2)}) copy-start(f32[4,64,256]{2,1,0:T(8,128)} %constant.6.clone.code_ref) | copy-start | bytes 786436
  7.0 0.9 %copy-start.5 = (bf16[256,256]{1,0:T(8,128)(2,1)S(1)}, bf16[256,256]{1,0:T(8,128)(2,1)}, u32[]{:S(2)}) copy-start(bf16[256,256]{1,0:T(8,128)(2,1)} %constant.8.clone.place_ref) | copy-start | bytes 393220
  7.9 0.9 %copy-start.6 = (bf16[256,256]{1,0:T(8,128)(2,1)S(1)}, bf16[256,256]{1,0:T(8,128)(2,1)}, u32[]{:S(2)}) copy-start(bf16[256,256]{1,0:T(8,128)(2,1)} %constant.7.clone.pick_ref) | copy-start | bytes 393220

commit v2 on v1

--- a/solution.py
+++ b/solution.py
@@ -63,7 +63,7 @@
                     codes[b, q, n] = 9
                 else:
                     codes[b, q, n] = (key[0] // LABEL - b + 1) * 3 + key[1] // LABEL + 1
-    return codes
+    return np.tile(codes.transpose(0, 2, 1), (1, 1, 2))
 
 
 def dot(a, b, contract):
@@ -72,10 +72,10 @@
 
 def kernel(
     sizes,
-    q_ref, k_ref, v_ref, do_ref, tissue_ref, slide_ref, code_ref, pick_ref, place_ref,
+    q_hbm, k_hbm, v_hbm, do_hbm, tissue_ref, slide_ref, code_hbm, pick_hbm, place_hbm,
     att_ref, dq_ref, dk_ref, dv_ref,
-    own, strip, edge, grow, gstrip, rrow, redge, acc, sacc, bias,
-    send_sem, recv_sem, gsend_sem, grecv_sem,
+    q_ref, do_ref, code_ref, pick_ref, place_ref, own, strip, edge, grow, gstrip, rrow, redge, acc, sacc, bias,
+    send_sem, recv_sem, gsend_sem, grecv_sem, load_sem, table_sem,
 ):
     rows, cols, groups, width, depth, row_size, col_size = sizes
     tokens = rows * cols
@@ -129,6 +129,27 @@
             src_ref=src, dst_ref=dst, send_sem=gsend_sem.at[g, n], recv_sem=grecv_sem.at[g, n],
             device_id=target, device_id_type=MESH)
 
+    def load(g, n):
+        lanes = pl.ds(g * width, width)
+        if n < 2:
+            src, dst = (k_hbm, v_hbm)[n], own.at[g, n, pl.ds(rim, tokens)]
+        else:
+            src, dst = (q_hbm, do_hbm)[n - 2], (q_ref, do_ref)[n - 2].at[g]
+        return pltpu.make_async_copy(src.at[:, lanes], dst, load_sem.at[g, n])
+
+    tables = [
+        pltpu.make_async_copy(src, dst, table_sem.at[n])
+        for n, (src, dst) in enumerate(((pick_hbm, pick_ref), (code_hbm, code_ref), (place_hbm, place_ref)))]
+    tables[0].start()
+    for g in range(groups):
+        for n in range(2):
+            load(g, n).start()
+    tables[1].start()
+    for g in range(groups):
+        for n in range(2, 4):
+            load(g, n).start()
+    tables[2].start()
+
     zero_rim = jnp.zeros((groups, 2, rim, width), BF16)
     own[:, :, pl.ds(0, rim)] = zero_rim
     own[:, :, pl.ds(rim + tokens, rim)] = zero_rim
@@ -148,35 +169,28 @@
                 def _(dr=dr, dc=dc):
                     pl.semaphore_signal(barrier, inc=1, device_id=device(dr, dc), device_id_type=MESH)
 
-    def stage(g, carry):
-        lanes = pl.ds(pl.multiple_of(g * width, width), width)
-        for i, ref in enumerate((k_ref, v_ref)):
-            block = ref[:, lanes]
-            own[g, i, pl.ds(rim, tokens)] = block
-            picked = dot(pick_ref[...], block, (1, 0)).astype(BF16)
+    tables[0].wait()
+    for g in range(groups):
+        for i in range(2):
+            load(g, i).wait()
+            picked = dot(pick_ref[...], own[g, i, pl.ds(rim, tokens)], (1, 0)).astype(BF16)
             edge[0, g, i] = picked[:slots]
             edge[1, g, i] = picked[slots:]
-        return carry
-
-    lax.fori_loop(0, groups, stage, 0)
-    pl.semaphore_wait(barrier, around)
-
-    def send(g, carry):
+        if g == 0:
+            pl.semaphore_wait(barrier, around)
         for n, (dr, dc, _, _) in enumerate(routes):
             @pl.when(exists(dr, dc))
             def _(n=n, dr=dr, dc=dc):
                 out_copy(g, n, device(dr, dc)).start()
-        return carry
-
-    lax.fori_loop(0, groups, send, 0)
 
     def label(r, c):
-        r_all, c_all = tissue_ref.shape
+        c_all, r_all = tissue_ref.shape
         inside = (r >= 0) & (r < r_all) & (c >= 0) & (c < c_all)
         r, c = jnp.clip(r, 0, r_all - 1), jnp.clip(c, 0, c_all - 1)
-        return jnp.where(inside & (tissue_ref[r, c] == 1), slide_ref[r, c] + 1, 0)
+        return jnp.where(inside & (tissue_ref[c, r] == 1), slide_ref[c, r] + 1, 0)
 
     labels = [[label(row * blocks + i - 1, col + j - 1) for j in range(3)] for i in range(blocks + 2)]
+    tables[1].wait()
     for b in range(blocks):
         code = code_ref[b]
         mine = labels[b + 1][1]
@@ -197,6 +211,11 @@
         for h in range(1, stacked):
             result = jnp.where(lane_head == h, full[h * per_block:(h + 1) * per_block], result)
         return result
+
+    for g in range(groups):
+        for n in range(2, 4):
+            load(g, n).wait()
+    tables[2].wait()
 
     def compute(g, carry):
         for n, (dr, dc, _, _) in enumerate(routes):
@@ -211,29 +230,23 @@
             near = pl.ds(b * per_block, 128)
             far = pl.ds(strip_start(b, rows), 64)
             scale = 1.0 / depth ** 0.5
-            q = stack((q_ref[mine, lanes].astype(F32) * scale).astype(BF16))
-            grad_block = do_ref[mine, lanes]
-            do = stack(grad_block)
+            q = stack((q_ref[g, mine].astype(F32) * scale).astype(BF16))
+            do = stack(do_ref[g, mine])
             keys, values = (
                 jnp.concatenate([own[g, i, near], strip[0, g, i, far], strip[1, g, i, far]], axis=0)
                 for i in range(2))
-            level = bias[b]
-            scores = dot(q, keys, (1, 1)) + jnp.concatenate([level] * stacked, axis=0)
-            highest = jnp.max(scores, axis=1, keepdims=True)
+            scores = dot(keys, q, (1, 1)) + jnp.concatenate([bias[b]] * (stacked // 2), axis=1)
+            highest = jnp.max(scores, axis=0, keepdims=True)
             powers = jnp.exp(scores - highest)
-            total = jnp.sum(powers, axis=1, keepdims=True)
+            total = jnp.sum(powers, axis=0, keepdims=True)
             weights = powers * (1.0 / total)
             soft = weights.astype(BF16)
-            attended = unstack(dot(soft, values, (1, 0))).astype(BF16)
-            att_ref[mine, lanes] = attended
-            product = grad_block.astype(F32) * attended.astype(F32)
-            delta = jnp.concatenate(
-                [jnp.sum(jnp.where(lane_head == h, product, 0.0), axis=1, keepdims=True) for h in range(stacked)],
-                axis=0)
-            prob_grad = dot(do, values, (1, 1))
+            prob_grad = dot(values, do, (1, 1))
+            delta = jnp.sum(weights * prob_grad, axis=0, keepdims=True)
             score_grad = (weights * (prob_grad - delta)).astype(BF16)
-            dq_ref[mine, lanes] = (unstack(dot(score_grad, keys, (1, 0))) * scale).astype(BF16)
-            for i, part in enumerate((dot(score_grad, q, (0, 0)), dot(soft, do, (0, 0)))):
+            att_ref[mine, lanes] = unstack(dot(soft, values, (0, 0))).astype(BF16)
+            dq_ref[mine, lanes] = (unstack(dot(score_grad, keys, (0, 0))) * scale).astype(BF16)
+            for i, part in enumerate((dot(score_grad, q, (1, 0)), dot(soft, do, (1, 0)))):
                 acc[g, i, near] += part[:128]
                 sacc[0, i, far] += part[128:192]
                 sacc[1, i, far] += part[192:]
@@ -268,6 +281,14 @@
         return carry
 
     lax.fori_loop(0, groups, finish, 0)
+
+
+def write_out(*refs):
+    copies = [pltpu.make_async_copy(refs[n], refs[4 + n], refs[8].at[n]) for n in range(4)]
+    for copy in copies:
+        copy.start()
+    for copy in copies:
+        copy.wait()
 
 
 def local(queries, key_states, value_states, out_grad, tissue, slide_id):
@@ -284,12 +305,19 @@
     flat = [a.reshape(tokens, feature) for a in (queries, key_states, value_states, out_grad)]
     vmem = pl.BlockSpec(memory_space=pltpu.VMEM)
     smem = pl.BlockSpec(memory_space=pltpu.SMEM)
+    hbm = pl.BlockSpec(memory_space=pltpu.HBM)
+    blocks = rows // LABEL
     outs = pl.pallas_call(
         functools.partial(kernel, sizes),
         out_shape=[jax.ShapeDtypeStruct((tokens, feature), BF16)] * 4,
-        in_specs=[vmem] * 4 + [smem] * 2 + [vmem] * 3,
+        in_specs=[hbm] * 4 + [smem] * 2 + [hbm] * 3,
         out_specs=[vmem] * 4,
         scratch_shapes=[
+            pltpu.VMEM((groups, tokens, width), BF16),
+            pltpu.VMEM((groups, tokens, width), BF16),
+            pltpu.VMEM((blocks, 256, 2 * LABEL * cols), F32),
+            pltpu.VMEM((2 * slots, tokens), BF16),
+            pltpu.VMEM((tokens, 2 * slots), BF16),
             pltpu.VMEM((groups, 2, tokens + 2 * rim, width), BF16),
             pltpu.VMEM((2, groups, 2, slots, width), BF16),
             pltpu.VMEM((2, groups, 2, slots, width), BF16),
@@ -299,21 +327,31 @@
             pltpu.VMEM((2, groups, 2, slots, width), BF16),
             pltpu.VMEM((groups, 2, tokens + 2 * rim, width), F32),
             pltpu.VMEM((2, 2, slots, width), F32),
-            pltpu.VMEM((rows // LABEL, LABEL * cols, 256), F32),
+            pltpu.VMEM((blocks, 256, 2 * LABEL * cols), F32),
             pltpu.SemaphoreType.DMA((groups, 8)),
             pltpu.SemaphoreType.DMA((groups, 8)),
             pltpu.SemaphoreType.DMA((groups, 8)),
             pltpu.SemaphoreType.DMA((groups, 8)),
+            pltpu.SemaphoreType.DMA((groups, 4)),
+            pltpu.SemaphoreType.DMA((3,)),
         ],
         compiler_params=pltpu.CompilerParams(
-            collective_id=0, has_side_effects=True, vmem_limit_bytes=48 * 2 ** 20),
+            collective_id=0, has_side_effects=True, vmem_limit_bytes=60 * 2 ** 20),
         name="window_attention",
     )(
-        *flat, tissue, slide_id,
+        *flat, tissue.T, slide_id.T,
         jnp.asarray(pair_codes(rows, cols)),
         jnp.asarray(picks, BF16),
         jnp.asarray(picks.T, BF16),
     )
+    outs = pl.pallas_call(
+        write_out,
+        out_shape=[jax.ShapeDtypeStruct((tokens, feature), BF16)] * 4,
+        in_specs=[pl.BlockSpec(memory_space=pl.ANY)] * 4,
+        out_specs=[hbm] * 4,
+        scratch_shapes=[pltpu.SemaphoreType.DMA((4,))],
+        name="write_out",
+    )(*outs)
     return tuple(a.reshape(rows, cols, feature) for a in outs)
 
 

time: 39.1 us -> 75 us (1.92)
  Pallas kernels: 26.6 us -> 73.9 us
  local copies, waits for them, and re-layouts: 11.2 us -> 0 us
    pallas_call x0 -> x1, Pallas kernels: none -> 48.8 us  [local(): pl.pallas_call(write_out, out_shape=[jax.ShapeDtypeStruct((tokens, featur...]
    unnamed x24 -> x0, local copies, waits for them, and re-layouts: 11.2 us -> none
    pallas_call x1, Pallas kernels: 26.6 us -> 25.1 us  [local(): pl.pallas_call(functools.partial(kernel, sizes), out_shape=[jax.ShapeDtyp...]
where the time goes in v2:
time: 75 us; the launch traced here: 74.5 us
  Pallas kernels  73.9 us (99%)
    pallas_call x1, Pallas kernels, local(): pl.pallas_call(write_out, out_shape=[jax.ShapeDtypeStruct((tokens, featur...  48.8 us
    pallas_call x1, Pallas kernels, local(): pl.pallas_call(functools.partial(kernel, sizes), out_shape=[jax.ShapeDtyp...  25.1 us

profile of v2, /device:TPU:1, one launch (start us, length us, event | category | flops | bytes accessed | tf_op | source)
XLA Modules:
  0.0 74.5 jit_solution(2316176378950861550)
XLA Ops:
  0.6 25.1 %window_attention.1 = (bf16[256,768]{1,0:T(8,128)(2,1)}, bf16[256,768]{1,0:T(8,128)(2,1)}, bf16[256,768]{1,0:T(8,128)(2,1)}, bf16[256,768]{1,0:T(8,128)(2,1)}) custom-call(bf16[256,768]{1,0:T(8,128)(2,1)} %bitcast.10, bf16[256,768]{1,0:T(8,128)(2,1)} %bitcast.11, bf16[256,768]{1,0:T(8,128)(2,1)} %bitcast.12, bf16[256,768]{1,0:T(8,128)(2,1)} %bitcast.13, ...), custom_call_target="tpu_custom_call" | custom-call | tf_op jit(solution)/shard_map/window_attention/pallas_call | solution.py:310
  25.7 48.8 %write_out.1 = (bf16[256,768]{1,0:T(8,128)(2,1)}, bf16[256,768]{1,0:T(8,128)(2,1)}, bf16[256,768]{1,0:T(8,128)(2,1)}, bf16[256,768]{1,0:T(8,128)(2,1)}) custom-call(bf16[256,768]{1,0:T(8,128)(2,1)} %get-tuple-element.12.refs_0_, bf16[256,768]{1,0:T(8,128)(2,1)} %get-tuple-element.13.refs_1_, bf16[256,768]{1,0:T(8,128)(2,1)} %get-tuple-element.14.refs_2_, ...), custom_call_target="tpu_custom_call" | custom-call | tf_op jit(solution)/shard_map/write_out/pallas_call | solution.py:347

commit v3 on v2

--- a/solution.py
+++ b/solution.py
@@ -72,9 +72,9 @@
 
 def kernel(
     sizes,
-    q_hbm, k_hbm, v_hbm, do_hbm, tissue_ref, slide_ref, code_hbm, pick_hbm, place_hbm,
+    q_hbm, k_hbm, v_hbm, do_hbm, tissue_hbm, slide_hbm, code_hbm, pick_hbm, place_hbm,
     att_ref, dq_ref, dk_ref, dv_ref,
-    q_ref, do_ref, code_ref, pick_ref, place_ref, own, strip, edge, grow, gstrip, rrow, redge, acc, sacc, bias,
+    tissue_ref, slide_ref, q_ref, do_ref, code_ref, pick_ref, place_ref, own, strip, edge, grow, gstrip, rrow, redge, acc, sacc, bias,
     send_sem, recv_sem, gsend_sem, grecv_sem, load_sem, table_sem,
 ):
     rows, cols, groups, width, depth, row_size, col_size = sizes
@@ -139,12 +139,14 @@
 
     tables = [
         pltpu.make_async_copy(src, dst, table_sem.at[n])
-        for n, (src, dst) in enumerate(((pick_hbm, pick_ref), (code_hbm, code_ref), (place_hbm, place_ref)))]
+        for n, (src, dst) in enumerate(((pick_hbm, pick_ref), (code_hbm, code_ref), (place_hbm, place_ref),
+                                        (tissue_hbm, tissue_ref), (slide_hbm, slide_ref)))]
     tables[0].start()
     for g in range(groups):
         for n in range(2):
             load(g, n).start()
-    tables[1].start()
+    for n in (1, 3, 4):
+        tables[n].start()
     for g in range(groups):
         for n in range(2, 4):
             load(g, n).start()
@@ -189,6 +191,8 @@
         r, c = jnp.clip(r, 0, r_all - 1), jnp.clip(c, 0, c_all - 1)
         return jnp.where(inside & (tissue_ref[c, r] == 1), slide_ref[c, r] + 1, 0)
 
+    tables[3].wait()
+    tables[4].wait()
     labels = [[label(row * blocks + i - 1, col + j - 1) for j in range(3)] for i in range(blocks + 2)]
     tables[1].wait()
     for b in range(blocks):
@@ -302,17 +306,18 @@
     slots = REACH * rows + 2 * PACK
     sizes = (rows, cols, groups, width, depth, lax.axis_size("row"), lax.axis_size("col"))
     picks = edge_picks(rows, cols)
-    flat = [a.reshape(tokens, feature) for a in (queries, key_states, value_states, out_grad)]
+    flat = [pltpu.with_memory_space_constraint(a.reshape(tokens, feature), pltpu.HBM) for a in (queries, key_states, value_states, out_grad)]
     vmem = pl.BlockSpec(memory_space=pltpu.VMEM)
-    smem = pl.BlockSpec(memory_space=pltpu.SMEM)
     hbm = pl.BlockSpec(memory_space=pltpu.HBM)
     blocks = rows // LABEL
     outs = pl.pallas_call(
         functools.partial(kernel, sizes),
-        out_shape=[jax.ShapeDtypeStruct((tokens, feature), BF16)] * 4,
-        in_specs=[hbm] * 4 + [smem] * 2 + [hbm] * 3,
+        out_shape=[pltpu.VMEM((tokens, feature), BF16)] * 4,
+        in_specs=[hbm] * 4 + [hbm] * 2 + [hbm] * 3,
         out_specs=[vmem] * 4,
         scratch_shapes=[
+            pltpu.SMEM(tissue.shape[::-1], jnp.int32),
+            pltpu.SMEM(tissue.shape[::-1], jnp.int32),
             pltpu.VMEM((groups, tokens, width), BF16),
             pltpu.VMEM((groups, tokens, width), BF16),
             pltpu.VMEM((blocks, 256, 2 * LABEL * cols), F32),
@@ -333,25 +338,26 @@
             pltpu.SemaphoreType.DMA((groups, 8)),
             pltpu.SemaphoreType.DMA((groups, 8)),
             pltpu.SemaphoreType.DMA((groups, 4)),
-            pltpu.SemaphoreType.DMA((3,)),
+            pltpu.SemaphoreType.DMA((5,)),
         ],
         compiler_params=pltpu.CompilerParams(
-            collective_id=0, has_side_effects=True, vmem_limit_bytes=60 * 2 ** 20),
+            collective_id=0, has_side_effects=True, vmem_limit_bytes=40 * 2 ** 20),
         name="window_attention",
     )(
-        *flat, tissue.T, slide_id.T,
-        jnp.asarray(pair_codes(rows, cols)),
+        *flat,
+        *[pltpu.with_memory_space_constraint(a.T, pltpu.HBM) for a in (tissue, slide_id)],
+        *[pltpu.with_memory_space_constraint(a, pltpu.HBM) for a in (jnp.asarray(pair_codes(rows, cols)),
         jnp.asarray(picks, BF16),
-        jnp.asarray(picks.T, BF16),
+        jnp.asarray(picks.T, BF16))],
     )
     outs = pl.pallas_call(
         write_out,
         out_shape=[jax.ShapeDtypeStruct((tokens, feature), BF16)] * 4,
-        in_specs=[pl.BlockSpec(memory_space=pl.ANY)] * 4,
+        in_specs=[vmem] * 4,
         out_specs=[hbm] * 4,
         scratch_shapes=[pltpu.SemaphoreType.DMA((4,))],
         name="write_out",
-    )(*outs)
+    )(*[pltpu.with_memory_space_constraint(a, pltpu.VMEM) for a in outs])
     return tuple(a.reshape(rows, cols, feature) for a in outs)
 
 

time: 75 us -> 25.4 us (0.34)
  Pallas kernels: 73.9 us -> 24.2 us
    pallas_call x1, Pallas kernels: 48.8 us -> 1.17 us  [local(): pl.pallas_call(write_out, out_shape=[jax.ShapeDtypeStruct((tokens, featur...]
    pallas_call x1, Pallas kernels: 25.1 us -> 23.1 us  [local(): pl.pallas_call(functools.partial(kernel, sizes), out_shape=[pltpu.VMEM((t...]
where the time goes in v3:
time: 25.4 us; the launch traced here: 24.9 us
  Pallas kernels  24.2 us (95%)
  between operations  0.64 us (3%)
    pallas_call x1, Pallas kernels, local(): pl.pallas_call(functools.partial(kernel, sizes), out_shape=[pltpu.VMEM((t...  23.1 us
    pallas_call x1, Pallas kernels, local(): pl.pallas_call(write_out, out_shape=[jax.ShapeDtypeStruct((tokens, featur...  1.17 us

profile of v3, /device:TPU:1, one launch (start us, length us, event | category | flops | bytes accessed | tf_op | source)
XLA Modules:
  0.0 24.9 jit_solution(12893679192165908936)
XLA Ops:
  0.6 23.1 %window_attention.1 = (bf16[256,768]{1,0:T(8,128)(2,1)S(1)}, bf16[256,768]{1,0:T(8,128)(2,1)S(1)}, bf16[256,768]{1,0:T(8,128)(2,1)S(1)}, bf16[256,768]{1,0:T(8,128)(2,1)S(1)}) custom-call(bf16[256,768]{1,0:T(8,128)(2,1)} %bitcast.10, bf16[256,768]{1,0:T(8,128)(2,1)} %bitcast.11, bf16[256,768]{1,0:T(8,128)(2,1)} %bitcast.12, bf16[256,768]{1,0:T(8,128)(2,1)} %bitcast.13, ...), custom_call_target="tpu_custom_call" | custom-call | tf_op jit(solution)/shard_map/window_attention/pallas_call | solution.py:313
  23.7 1.2 %write_out.1 = (bf16[256,768]{1,0:T(8,128)(2,1)}, bf16[256,768]{1,0:T(8,128)(2,1)}, bf16[256,768]{1,0:T(8,128)(2,1)}, bf16[256,768]{1,0:T(8,128)(2,1)}) custom-call(bf16[256,768]{1,0:T(8,128)(2,1)S(1)} %get-tuple-element.12.refs_0_, bf16[256,768]{1,0:T(8,128)(2,1)S(1)} %get-tuple-element.13.refs_1_, bf16[256,768]{1,0:T(8,128)(2,1)S(1)} %get-tuple-element.14.refs_2_, ...), custom_call_target="tpu_custom_call" | custom-call | tf_op jit(solution)/shard_map/write_out/pallas_call | solution.py:353

commit v4 on v3

--- a/solution.py
+++ b/solution.py
@@ -89,12 +89,13 @@
 
     top, mid, bottom = pl.ds(0, PACK), pl.ds(PACK, side), pl.ds(PACK + side, PACK)
     routes = []
+    routes.append((-1, 0, 2, None))
+    routes.append((1, 0, 3, None))
     for source, dc in ((0, -1), (1, 1)):
-        routes.append((0, dc, source, mid))
         routes.append((1, dc, source, top))
         routes.append((-1, dc, source, bottom))
-    routes.append((-1, 0, 2, None))
-    routes.append((1, 0, 3, None))
+    routes.append((0, -1, 0, mid))
+    routes.append((0, 1, 1, mid))
 
     def exists(dr, dc):
         good = None
@@ -222,14 +223,21 @@
     tables[2].wait()
 
     def compute(g, carry):
-        for n, (dr, dc, _, _) in enumerate(routes):
-            @pl.when(exists(-dr, -dc))
-            def _(n=n, dr=dr, dc=dc):
-                out_copy(g, n, device(-dr, -dc)).wait_recv()
+        for n, (dr, dc, _, part) in enumerate(routes):
+            if part is mid:
+                @pl.when(exists(-dr, -dc))
+                def _(n=n, dr=dr, dc=dc):
+                    out_copy(g, n, device(-dr, -dc)).wait_recv()
         lanes = pl.ds(pl.multiple_of(g * width, width), width)
         acc[g] = jnp.zeros(acc.shape[1:], F32)
         sacc[...] = jnp.zeros(sacc.shape, F32)
-        for b in range(blocks):
+        for b in [*range(1, blocks - 1), blocks - 1, 0]:
+            if b == blocks - 1:
+                for n, (dr, dc, _, part) in enumerate(routes):
+                    if part is not mid:
+                        @pl.when(exists(-dr, -dc))
+                        def _(n=n, dr=dr, dc=dc):
+                            out_copy(g, n, device(-dr, -dc)).wait_recv()
             mine = pl.ds(b * per_block, per_block)
             near = pl.ds(b * per_block, 128)
             far = pl.ds(strip_start(b, rows), 64)

time: 25.4 us -> 24.7 us (0.972); the launches traced: 24.9 us -> 24.6 us
  Pallas kernels: 24.2 us -> 23.9 us
    pallas_call x1, Pallas kernels: 23.1 us -> 22.7 us  [local(): pl.pallas_call(functools.partial(kernel, sizes), out_shape=[pltpu.VMEM((t...]
where the time goes in v4:
time: 24.7 us; the launch traced here: 24.6 us
  Pallas kernels  23.9 us (97%)
  between operations  0.64 us (3%)
    pallas_call x1, Pallas kernels, local(): pl.pallas_call(functools.partial(kernel, sizes), out_shape=[pltpu.VMEM((t...  22.7 us
    pallas_call x1, Pallas kernels, local(): pl.pallas_call(write_out, out_shape=[jax.ShapeDtypeStruct((tokens, featur...  1.17 us

profile of v4, /device:TPU:1, one launch (start us, length us, event | category | flops | bytes accessed | tf_op | source)
XLA Modules:
  0.0 24.6 jit_solution(11480972447425038953)
XLA Ops:
  0.6 22.7 %window_attention.1 = (bf16[256,768]{1,0:T(8,128)(2,1)S(1)}, bf16[256,768]{1,0:T(8,128)(2,1)S(1)}, bf16[256,768]{1,0:T(8,128)(2,1)S(1)}, bf16[256,768]{1,0:T(8,128)(2,1)S(1)}) custom-call(bf16[256,768]{1,0:T(8,128)(2,1)} %bitcast.10, bf16[256,768]{1,0:T(8,128)(2,1)} %bitcast.11, bf16[256,768]{1,0:T(8,128)(2,1)} %bitcast.12, bf16[256,768]{1,0:T(8,128)(2,1)} %bitcast.13, ...), custom_call_target="tpu_custom_call" | custom-call | tf_op jit(solution)/shard_map/window_attention/pallas_call | solution.py:321
  23.4 1.2 %write_out.1 = (bf16[256,768]{1,0:T(8,128)(2,1)}, bf16[256,768]{1,0:T(8,128)(2,1)}, bf16[256,768]{1,0:T(8,128)(2,1)}, bf16[256,768]{1,0:T(8,128)(2,1)}) custom-call(bf16[256,768]{1,0:T(8,128)(2,1)S(1)} %get-tuple-element.12.refs_0_, bf16[256,768]{1,0:T(8,128)(2,1)S(1)} %get-tuple-element.13.refs_1_, bf16[256,768]{1,0:T(8,128)(2,1)S(1)} %get-tuple-element.14.refs_2_, ...), custom_call_target="tpu_custom_call" | custom-call | tf_op jit(solution)/shard_map/write_out/pallas_call | solution.py:361
